TPU v7x, 512 devices: a whole 4x4x16 slice. The times are simulated.
512 devices in a mesh: pix: 64 (over z, y_lo, core), tm: 8 (over y_hi, x).
Axes of the slice: x: 4, y: 4 (y_hi: 2, y_lo: 2; y = y_hi * 2 + y_lo), z: 16, core: 2. Of those that a mesh axis runs over, the one named last changes fastest.
Arguments:
- signal: bfloat16 [16384, 16, 256], P('pix', 'tm'), may hold values from -6 to 6
- lap_tiles: bfloat16 [256, 9, 64, 64], P('pix'), may hold values from -0.25 to 0.25
- neighbours: int32 [256, 9], replicated, may hold values from 0 to 255, as said below
- cheb_weight: bfloat16 [3, 256, 256], replicated, may hold values from -0.21875 to 0.21875
- norm_gain: float32 [256], replicated, may hold values from 0.25 to 1.75
- w_query: bfloat16 [256, 256], replicated, may hold values from -6.5 to 6.5
- w_key: bfloat16 [256, 256], replicated, may hold values from -0.375 to 0.375
- w_value: bfloat16 [256, 256], replicated, may hold values from -0.375 to 0.375
- w_out: bfloat16 [256, 256], replicated, may hold values from -0.375 to 0.375
Outputs:
- result: bfloat16 [16384, 16, 256], P('pix', 'tm')
Inputs may be any that keep to these rules, and one draw needn't show every extreme that they name: `neighbours`: row g lists blocks g - 2, g - 1, g, g + 1, g + 2 in its first five entries (g itself where one of them does not exist); each of the other four entries is one of those five.
All inputs are finite; a program needn't handle non-finite values.
Results may differ from a plain program's by a relative error of at most 0.017.
Values may be sent and summed in bfloat16 or wider, within the bound.
A program may use at most 64 MiB of HBM per device.

v0:
```python
from functools import partial
import math

import jax
import jax.numpy as jnp
from jax import lax
from jax.sharding import PartitionSpec as P

HEADS = 8


reach_blocks = 2


def with_halo(block, sides, width):
    for axis, dim in sides:
        count = lax.axis_size(axis)
        forward = [(i, i + 1) for i in range(count - 1)]
        backward = [(target, source) for source, target in forward]
        low = lax.ppermute(
            lax.slice_in_dim(block, block.shape[dim] - width, None, axis=dim), axis, forward
        )
        high = lax.ppermute(lax.slice_in_dim(block, 0, width, axis=dim), axis, backward)
        block = jnp.concatenate([low, block, high], axis=dim)
    return block


def apply_tiles(tile_blocks, source, sources_at):
    summed = None
    for slot in range(tile_blocks.shape[1]):
        chosen = jnp.take(source, sources_at[:, slot], axis=0, mode="clip")
        product = jnp.einsum(
            "gab,gbf->gaf", tile_blocks[:, slot], chosen, preferred_element_type=jnp.float32
        )
        summed = product if summed is None else summed + product
    return summed


def attend_group(grouped, norm_gain, w_query, w_key, w_value, w_out):
    block = grouped[0]
    count, times, channels = block.shape
    head_dim = channels // HEADS
    flat = block.reshape(count * times, channels).astype(jnp.float32)
    scaling = lax.rsqrt(jnp.mean(flat * flat, axis=1, keepdims=True) + 1e-06)
    normed = (flat * scaling * norm_gain[None, :]).astype(jnp.bfloat16)
    query = jnp.dot(normed, w_query, preferred_element_type=jnp.float32).astype(jnp.bfloat16)
    keys = jnp.dot(normed, w_key, preferred_element_type=jnp.float32).astype(jnp.bfloat16)
    values = jnp.dot(normed, w_value, preferred_element_type=jnp.float32).astype(jnp.bfloat16)
    query = query.reshape(count, times, HEADS, head_dim)
    keys = keys.reshape(count, times, HEADS, head_dim)
    values = values.reshape(count, times, HEADS, head_dim)
    scores = jnp.einsum(
        "pshd,pthd->phst", query, keys, preferred_element_type=jnp.float32
    ) / math.sqrt(head_dim)
    weights = jax.nn.softmax(scores, axis=-1).astype(jnp.bfloat16)
    attended = jnp.einsum(
        "phst,pthd->pshd", weights, values, preferred_element_type=jnp.float32
    ).astype(jnp.bfloat16)
    attended = attended.reshape(count * times, channels)
    output = flat + jnp.dot(attended, w_out, preferred_element_type=jnp.float32)
    return output.astype(jnp.bfloat16).reshape(1, count, times, channels)


def on_device(
    signal, lap_tiles, neighbours, cheb_weight, norm_gain, w_query, w_key, w_value, w_out
):
    pix_count, time_count, channels = signal.shape
    block_count = lap_tiles.shape[0]
    tile_size = lap_tiles.shape[2]
    features = time_count * channels
    blocks = signal.reshape(block_count, tile_size, features)
    first_block = lax.axis_index("pix") * block_count
    own_rows = lax.dynamic_slice_in_dim(neighbours, first_block, block_count, 0)
    sources_at = own_rows - first_block + reach_blocks
    extended = with_halo(blocks, (("pix", 0),), 2)
    first_order = apply_tiles(lap_tiles, extended, sources_at).astype(jnp.bfloat16)
    first_wide = with_halo(first_order, (("pix", 0),), 2)
    second_order = (
        2.0 * apply_tiles(lap_tiles, first_wide, sources_at) - blocks.astype(jnp.float32)
    ).astype(jnp.bfloat16)
    row_count = pix_count * time_count
    plain = signal.reshape(row_count, channels)
    stacked = jnp.concatenate(
        [
            plain,
            first_order.reshape(row_count, channels),
            second_order.reshape(row_count, channels),
        ],
        axis=1,
    )
    mixing = jnp.dot(
        stacked, cheb_weight.reshape(3 * channels, channels), preferred_element_type=jnp.float32
    )
    mixed = (plain.astype(jnp.float32) + jax.nn.silu(mixing)).astype(jnp.bfloat16)
    group_count = lax.axis_size("tm")
    grouped = mixed.reshape(group_count, pix_count // group_count, time_count, channels)
    attend_fn = partial(
        attend_group,
        norm_gain=norm_gain,
        w_query=w_query,
        w_key=w_key,
        w_value=w_value,
        w_out=w_out,
    )
    attended = attend_fn(lax.all_to_all(grouped, "tm", split_axis=0, concat_axis=2, tiled=True))
    returned = lax.all_to_all(attended, "tm", split_axis=2, concat_axis=0, tiled=True)
    return returned.reshape(pix_count, time_count, channels)


def solution(mesh):
    in_specs = (P("pix", "tm", None), P("pix", None, None, None), P(), P(), P(), P(), P(), P(), P())
    out_specs = P("pix", "tm", None)
    return jax.shard_map(
        on_device, mesh=mesh, in_specs=in_specs, out_specs=out_specs, check_vma=False
    )
```

profile of v0, /device:TPU:105, one launch (start us, length us, event | category | flops | bytes accessed | tf_op | source)
XLA Modules:
  0.0 98.8 jit_solution(3153955818766768114)
XLA Ops:
  0.0 1.2 %fusion.106 = (bf16[128,2,256]{2,1,0:T(2,128)(2,1)S(1)}, bf16[128,2,256]{2,1,0:T(2,128)(2,1)S(1)}) fusion(bf16[256,2,256]{2,1,0:T(2,128)(2,1)} %param.9), kind=kLoop, calls=%fused_computation.148 | loop fusion | bytes 524288 | tf_op jit(solution)/shard_map/slice | solution.py:23
  1.3 5.2 %collective-permute-start = (bf16[2,64,512]{2,1,0:T(8,128)(2,1)S(1)}, bf16[2,64,512]{2,1,0:T(8,128)(2,1)S(1)}, u32[]{:S(2)}, u32[]{:S(2)}) collective-permute-start(bf16[2,64,512]{2,1,0:T(8,128)(2,1)S(1)} %slice.91), channel_id=1, source_target_pairs={{0,8},{8,16},{16,24},{24,32},{32,40},{40,48},{48,56},{56,64},{64,7... | collective-permute-start | bytes 393224 | tf_op jit(solution)/shard_map/ppermute | solution.py:20
  6.6 1.9 %collective-permute-start.1 = (bf16[2,64,512]{2,1,0:T(8,128)(2,1)S(1)}, bf16[2,64,512]{2,1,0:T(8,128)(2,1)S(1)}, u32[]{:S(2)}, u32[]{:S(2)}) collective-permute-start(bf16[2,64,512]{2,1,0:T(8,128)(2,1)S(1)} %slice.93), channel_id=1, source_target_pairs={{8,0},{16,8},{24,16},{32,24},{40,32},{48,40},{56,48},{64,56},{72,6... | collective-permute-start | bytes 393224 | tf_op jit(solution)/shard_map/ppermute | solution.py:23
  8.6 0.8 subtract_add_fusion
  9.4 1.1 %reshape.67 = bf16[4,64,512]{2,1,0:T(8,128)(2,1)S(1)} reshape(bf16[256,2,256]{2,1,0:T(2,128)(2,1)} %param.9) | data formatting | bytes 524288 | tf_op jit(solution)/shard_map/reshape | solution.py:71
  10.6 4.4 %collective-permute-done.1 = bf16[2,64,512]{2,1,0:T(8,128)(2,1)S(1)} collective-permute-done((bf16[2,64,512]{2,1,0:T(8,128)(2,1)S(1)}, bf16[2,64,512]{2,1,0:T(8,128)(2,1)S(1)}, u32[]{:S(2)}, u32[]{:S(2)}) %collective-permute-start.1) | collective-permute-done | bytes 131104 | tf_op jit(solution)/shard_map/ppermute | solution.py:23
  15.1 0.6 gather_fusion.7
  15.6 0.6 gather_fusion.6
  16.2 0.2 fusion.43
  16.4 0.2 fusion.47
  16.6 1.3 %gather_fusion.5 = bf16[4,64,512]{2,1,0:T(8,128)(2,1)} fusion(bf16[8,64,512]{2,1,0:T(8,128)(2,1)S(1)} %constant_dynamic-update-slice_fusion, s32[1024]{0:T(1024)S(1)} %get-tuple-element.23), kind=kCustom, calls=%fused_computation.5 | custom fusion | bytes 524304 | tf_op jit(solution)/shard_map/jit(_take)/gather | solution.py:31
  17.9 1.1 %fusion.51 = f32[4,512,64]{1,2,0:T(8,128)S(1)} fusion(bf16[4,64,512]{2,1,0:T(8,128)(2,1)} %gather_fusion.5, bf16[4,9,64,64]{3,2,1,0:T(8,128)(2,1)S(1)} %copy-done.2), kind=kOutput, calls=%fused_computation.82 | convolution fusion | flops 16777216 | bytes 851968 | tf_op jit(solution)/shard_map/gab,gbf->gaf/dot_general | solution.py:32
  19.0 1.3 %gather_fusion.4 = bf16[4,64,512]{2,1,0:T(8,128)(2,1)} fusion(bf16[8,64,512]{2,1,0:T(8,128)(2,1)S(1)} %constant_dynamic-update-slice_fusion, s32[1024]{0:T(1024)S(1)} %get-tuple-element.24), kind=kCustom, calls=%fused_computation.4 | custom fusion | bytes 524304 | tf_op jit(solution)/shard_map/jit(_take)/gather | solution.py:31
  20.3 1.9 %fusion.55 = f32[4,512,64]{1,2,0:T(8,128)} fusion(bf16[4,64,512]{2,1,0:T(8,128)(2,1)} %gather_fusion.4, bf16[4,9,64,64]{3,2,1,0:T(8,128)(2,1)S(1)} %copy-done.2), kind=kOutput, calls=%fused_computation.86 | convolution fusion | flops 16777216 | bytes 851968 | tf_op jit(solution)/shard_map/gab,gbf->gaf/dot_general | solution.py:32
  22.3 1.3 %gather_fusion.3 = bf16[4,64,512]{2,1,0:T(8,128)(2,1)} fusion(bf16[8,64,512]{2,1,0:T(8,128)(2,1)S(1)} %constant_dynamic-update-slice_fusion, s32[1024]{0:T(1024)S(1)} %get-tuple-element.25), kind=kCustom, calls=%fused_computation.3 | custom fusion | bytes 524304 | tf_op jit(solution)/shard_map/jit(_take)/gather | solution.py:31
  23.5 2.0 %fusion.59 = f32[4,512,64]{1,2,0:T(8,128)} fusion(bf16[4,64,512]{2,1,0:T(8,128)(2,1)} %gather_fusion.3, bf16[4,9,64,64]{3,2,1,0:T(8,128)(2,1)S(1)} %copy-done.2), kind=kOutput, calls=%fused_computation.90 | convolution fusion | flops 16777216 | bytes 851968 | tf_op jit(solution)/shard_map/gab,gbf->gaf/dot_general | solution.py:32
  25.5 1.3 %gather_fusion.2 = bf16[4,64,512]{2,1,0:T(8,128)(2,1)} fusion(bf16[8,64,512]{2,1,0:T(8,128)(2,1)S(1)} %constant_dynamic-update-slice_fusion, s32[1024]{0:T(1024)S(1)} %get-tuple-element.26), kind=kCustom, calls=%fused_computation.2 | custom fusion | bytes 524304 | tf_op jit(solution)/shard_map/jit(_take)/gather | solution.py:31
  26.8 2.0 %fusion.63 = f32[4,512,64]{1,2,0:T(8,128)} fusion(bf16[4,64,512]{2,1,0:T(8,128)(2,1)} %gather_fusion.2, bf16[4,9,64,64]{3,2,1,0:T(8,128)(2,1)S(1)} %copy-done.2), kind=kOutput, calls=%fused_computation.94 | convolution fusion | flops 16777216 | bytes 851968 | tf_op jit(solution)/shard_map/gab,gbf->gaf/dot_general | solution.py:32
  28.7 1.3 %gather_fusion.1 = bf16[4,64,512]{2,1,0:T(8,128)(2,1)} fusion(bf16[8,64,512]{2,1,0:T(8,128)(2,1)S(1)} %constant_dynamic-update-slice_fusion, s32[1024]{0:T(1024)S(1)} %get-tuple-element.27), kind=kCustom, calls=%fused_computation.1 | custom fusion | bytes 524304 | tf_op jit(solution)/shard_map/jit(_take)/gather | solution.py:31
  30.0 2.0 %fusion.67 = f32[4,512,64]{1,2,0:T(8,128)} fusion(bf16[4,64,512]{2,1,0:T(8,128)(2,1)} %gather_fusion.1, bf16[4,9,64,64]{3,2,1,0:T(8,128)(2,1)S(1)} %copy-done.2), kind=kOutput, calls=%fused_computation.98 | convolution fusion | flops 16777216 | bytes 851968 | tf_op jit(solution)/shard_map/gab,gbf->gaf/dot_general | solution.py:32
  32.0 1.3 %gather_fusion.8 = bf16[4,64,512]{2,1,0:T(8,128)(2,1)} fusion(bf16[8,64,512]{2,1,0:T(8,128)(2,1)S(1)} %constant_dynamic-update-slice_fusion, s32[1024]{0:T(1024)S(1)} %get-tuple-element.20), kind=kCustom, calls=%fused_computation.8 | custom fusion | bytes 524304 | tf_op jit(solution)/shard_map/jit(_take)/gather | solution.py:31
  33.2 2.0 %fusion.39 = f32[4,512,64]{1,2,0:T(8,128)} fusion(bf16[4,64,512]{2,1,0:T(8,128)(2,1)} %gather_fusion.8, bf16[4,9,64,64]{3,2,1,0:T(8,128)(2,1)S(1)} %copy-done.2), kind=kOutput, calls=%fused_computation.70 | convolution fusion | flops 16777216 | bytes 851968 | tf_op jit(solution)/shard_map/gab,gbf->gaf/dot_general | solution.py:32
  35.2 1.3 %gather_fusion = bf16[4,64,512]{2,1,0:T(8,128)(2,1)} fusion(bf16[8,64,512]{2,1,0:T(8,128)(2,1)S(1)} %constant_dynamic-update-slice_fusion, s32[1024]{0:T(1024)S(1)} %pad_clamp_fusion.8), kind=kCustom, calls=%fused_computation | custom fusion | bytes 524304 | tf_op jit(solution)/shard_map/jit(_take)/gather | solution.py:31
  36.5 2.1 %fusion.23 = bf16[4,64,512]{2,1,0:T(8,128)(2,1)S(1)} fusion(f32[4,512,64]{1,2,0:T(8,128)} %fusion.39, f32[4,512,64]{1,2,0:T(8,128)S(1)} %fusion.43, f32[4,512,64]{1,2,0:T(8,128)S(1)} %fusion.47, f32[4,512,64]{1,2,0:T(8,128)S(1)} %fusion.51, f32[4,512,64]{1,2,0:T(8,128)} %fusion.55, f32[4,512,64]{1,2,0:T(8,128)} %fusion.59, f32[4,512,64]{1,2,0:T(8,128)} %fusion.63, ...), kind=kOutput, calls=%fused_computation.51 | convolution fusion | flops 17956864 | bytes 4784128 | tf_op jit(solution)/shard_map/gab,gbf->gaf/dot_general | solution.py:32
  38.6 1.9 %collective-permute-start.2 = (bf16[2,64,512]{2,1,0:T(8,128)(2,1)S(1)}, bf16[2,64,512]{2,1,0:T(8,128)(2,1)S(1)}, u32[]{:S(2)}, u32[]{:S(2)}) collective-permute-start(bf16[2,64,512]{2,1,0:T(8,128)(2,1)S(1)} %get-tuple-element.5), channel_id=1, source_target_pairs={{0,8},{8,16},{16,24},{24,32},{32,40},{40,48},{48,56},{56,64},{64,7... | collective-permute-start | bytes 393224 | tf_op jit(solution)/shard_map/ppermute | solution.py:20
  40.5 2.4 %collective-permute-start.3 = (bf16[2,64,512]{2,1,0:T(8,128)(2,1)S(1)}, bf16[2,64,512]{2,1,0:T(8,128)(2,1)S(1)}, u32[]{:S(2)}, u32[]{:S(2)}) collective-permute-start(bf16[2,64,512]{2,1,0:T(8,128)(2,1)S(1)} %get-tuple-element.6), channel_id=1, source_target_pairs={{8,0},{16,8},{24,16},{32,24},{40,32},{48,40},{56,48},{64,56},{72,6... | collective-permute-start | bytes 393224 | tf_op jit(solution)/shard_map/ppermute | solution.py:23
  43.0 0.8 reshape.66
  43.8 0.8 reshape.68
  44.5 4.4 %collective-permute-done.3 = bf16[2,64,512]{2,1,0:T(8,128)(2,1)S(1)} collective-permute-done((bf16[2,64,512]{2,1,0:T(8,128)(2,1)S(1)}, bf16[2,64,512]{2,1,0:T(8,128)(2,1)S(1)}, u32[]{:S(2)}, u32[]{:S(2)}) %collective-permute-start.3) | collective-permute-done | bytes 131104 | tf_op jit(solution)/shard_map/ppermute | solution.py:23
  49.0 0.6 gather_fusion.16
  49.6 0.6 gather_fusion.15
  50.1 0.6 gather_fusion.14
  50.7 0.6 gather_fusion.13
  51.3 0.6 gather_fusion.12
  51.9 1.3 %gather_fusion.11 = bf16[4,64,512]{2,1,0:T(8,128)(2,1)} fusion(bf16[8,64,512]{2,1,0:T(8,128)(2,1)S(1)} %pad_maximum_fusion, s32[1024]{0:T(1024)S(1)} %get-tuple-element.26), kind=kCustom, calls=%fused_computation.11 | custom fusion | bytes 524304 | tf_op jit(solution)/shard_map/jit(_take)/gather | solution.py:31
  53.1 1.3 %gather_fusion.10 = bf16[4,64,512]{2,1,0:T(8,128)(2,1)} fusion(bf16[8,64,512]{2,1,0:T(8,128)(2,1)S(1)} %pad_maximum_fusion, s32[1024]{0:T(1024)S(1)} %get-tuple-element.27), kind=kCustom, calls=%fused_computation.10 | custom fusion | bytes 524304 | tf_op jit(solution)/shard_map/jit(_take)/gather | solution.py:31
  54.4 1.3 %gather_fusion.17 = bf16[4,64,512]{2,1,0:T(8,128)(2,1)} fusion(bf16[8,64,512]{2,1,0:T(8,128)(2,1)S(1)} %pad_maximum_fusion, s32[1024]{0:T(1024)S(1)} %get-tuple-element.20), kind=kCustom, calls=%fused_computation.17 | custom fusion | bytes 524304 | tf_op jit(solution)/shard_map/jit(_take)/gather | solution.py:31
  55.7 0.6 gather_fusion.9
  56.2 0.2 fusion.45
  56.4 0.2 fusion.49
  56.7 0.2 fusion.53
  56.9 0.2 fusion.57
  57.1 0.2 fusion.61
  57.3 0.2 fusion.65
  57.9 0.3 fusion.21
  58.4 0.5 copy-done.6
  59.0 0.4 add_convert_fusion
  59.5 13.5 %all_to_all.24 = bf16[8,32,2,256]{3,2,1,0:T(2,128)(2,1)S(1)} all-to-all(bf16[8,32,2,256]{3,2,1,0:T(2,128)(2,1)S(1)} %reshape.71), channel_id=1, replica_groups=mesh['pix'=64,'tm'=8] {'tm'}, dimensions={0} | all-to-all | bytes 524288 | tf_op jit(solution)/shard_map/all_to_all | solution.py:105
  73.2 0.3 copy.68
  73.5 0.4 reshape.78
  73.8 0.3 fusion.36
  74.8 0.2 convolution_convert_fusion.2
  75.0 0.4 reshape.73
  75.5 0.9 convolution_convert_fusion.1
  76.4 1.7 %reshape.74 = bf16[32,16,8,32]{3,2,1,0:T(8,128)(2,1)S(1)} reshape(bf16[512,256]{1,0:T(8,128)(2,1)} %convolution_convert_fusion.1) | data formatting | bytes 524288 | tf_op jit(solution)/shard_map/reshape | solution.py:50
  78.1 0.9 convolution_convert_fusion.3
  79.0 2.4 %reshape.72 = bf16[32,16,8,32]{3,2,1,0:T(8,128)(2,1)} reshape(bf16[512,256]{1,0:T(8,128)(2,1)} %convolution_convert_fusion.3) | data formatting | bytes 524288 | tf_op jit(solution)/shard_map/reshape | solution.py:51
  81.4 2.6 %fusion.107 = (f32[32,8,16]{2,1,0:T(8,128)S(1)}, f32[32,8,16,16]{2,3,1,0:T(8,128)}) fusion(bf16[32,16,8,32]{3,2,1,0:T(8,128)(2,1)S(1)} %reshape.74, bf16[32,16,8,32]{3,2,1,0:T(8,128)(2,1)S(1)} %reshape.73), kind=kOutput, calls=%fused_computation.149 | convolution fusion | flops 4390927 | bytes 802816 | tf_op jit(solution)/shard_map/sub | solution.py:55
  84.0 2.5 %fusion.2 = bf16[32,16,8,32]{3,1,2,0:T(8,128)(2,1)S(1)} fusion(f32[32,8,16,16]{2,3,1,0:T(8,128)} %get-tuple-element.19, bf16[32,16,8,32]{3,2,1,0:T(8,128)(2,1)} %reshape.72, f32[32,8,16]{2,1,0:T(8,128)S(1)} %get-tuple-element.18), kind=kOutput, calls=%fused_computation.24 | convolution fusion | flops 4456448 | bytes 802816 | tf_op jit(solution)/shard_map/phst,pthd->pshd/dot_general | solution.py:56
  86.5 0.3 copy.75
  86.8 0.7 reshape.75
  87.5 0.2 fusion.22
  87.8 10.1 %all_to_all.25 = bf16[1,32,16,256]{3,1,0,2:T(8,128)(2,1)S(1)} all-to-all(bf16[1,32,16,256]{3,1,0,2:T(8,128)(2,1)S(1)} %copy.76), channel_id=1, replica_groups=mesh['pix'=64,'tm'=8] {'tm'}, dimensions={2} | all-to-all | bytes 524288 | tf_op jit(solution)/shard_map/all_to_all | solution.py:106
  97.9 1.0 copy.77
  (51 shorter events, 1.9 us)
Async XLA Ops:
  0.0 58.4 %copy-start = (bf16[3,256,256]{2,1,0:T(8,128)(2,1)S(1)}, bf16[3,256,256]{2,1,0:T(8,128)(2,1)}, u32[]{:S(2)}) copy-start(bf16[3,256,256]{2,1,0:T(8,128)(2,1)} %param.12) | copy-start | bytes 1179652
  0.0 16.2 %copy-start.2 = (bf16[4,9,64,64]{3,2,1,0:T(8,128)(2,1)S(1)}, bf16[4,9,64,64]{3,2,1,0:T(8,128)(2,1)}, u32[]{:S(2)}) copy-start(bf16[4,9,64,64]{3,2,1,0:T(8,128)(2,1)} %param.10) | copy-start | bytes 884740
  1.3 9.2 %collective-permute-start = (bf16[2,64,512]{2,1,0:T(8,128)(2,1)S(1)}, bf16[2,64,512]{2,1,0:T(8,128)(2,1)S(1)}, u32[]{:S(2)}, u32[]{:S(2)}) collective-permute-start(bf16[2,64,512]{2,1,0:T(8,128)(2,1)S(1)} %slice.91), channel_id=1, source_target_pairs={{0,8},{8,16},{16,24},{24,32},{32,40},{40,48},{48,56},{56,64},{64,7... | collective-permute-start | bytes 393224 | tf_op jit(solution)/shard_map/ppermute | solution.py:20
  6.6 8.4 %collective-permute-start.1 = (bf16[2,64,512]{2,1,0:T(8,128)(2,1)S(1)}, bf16[2,64,512]{2,1,0:T(8,128)(2,1)S(1)}, u32[]{:S(2)}, u32[]{:S(2)}) collective-permute-start(bf16[2,64,512]{2,1,0:T(8,128)(2,1)S(1)} %slice.93), channel_id=1, source_target_pairs={{8,0},{16,8},{24,16},{32,24},{40,32},{48,40},{56,48},{64,56},{72,6... | collective-permute-start | bytes 393224 | tf_op jit(solution)/shard_map/ppermute | solution.py:23
  36.5 6.5 %copy-start.1 = (bf16[256,2,256]{2,1,0:T(2,128)(2,1)S(1)}, bf16[256,2,256]{2,1,0:T(2,128)(2,1)}, u32[]{:S(2)}) copy-start(bf16[256,2,256]{2,1,0:T(2,128)(2,1)} %param.9) | copy-start | bytes 786436
  38.6 5.9 %collective-permute-start.2 = (bf16[2,64,512]{2,1,0:T(8,128)(2,1)S(1)}, bf16[2,64,512]{2,1,0:T(8,128)(2,1)S(1)}, u32[]{:S(2)}, u32[]{:S(2)}) collective-permute-start(bf16[2,64,512]{2,1,0:T(8,128)(2,1)S(1)} %get-tuple-element.5), channel_id=1, source_target_pairs={{0,8},{8,16},{16,24},{24,32},{32,40},{40,48},{48,56},{56,64},{64,7... | collective-permute-start | bytes 393224 | tf_op jit(solution)/shard_map/ppermute | solution.py:20
  40.5 8.4 %collective-permute-start.3 = (bf16[2,64,512]{2,1,0:T(8,128)(2,1)S(1)}, bf16[2,64,512]{2,1,0:T(8,128)(2,1)S(1)}, u32[]{:S(2)}, u32[]{:S(2)}) collective-permute-start(bf16[2,64,512]{2,1,0:T(8,128)(2,1)S(1)} %get-tuple-element.6), channel_id=1, source_target_pairs={{8,0},{16,8},{24,16},{32,24},{40,32},{48,40},{56,48},{64,56},{72,6... | collective-permute-start | bytes 393224 | tf_op jit(solution)/shard_map/ppermute | solution.py:23
  56.2 1.1 %copy-start.3 = (bf16[4,64,512]{2,1,0:T(8,128)(2,1)S(1)}, bf16[4,64,512]{2,1,0:T(8,128)(2,1)}, u32[]{:S(2)}) copy-start(bf16[4,64,512]{2,1,0:T(8,128)(2,1)} %gather_fusion.11) | copy-start | bytes 786436
  56.4 1.1 %copy-start.4 = (bf16[4,64,512]{2,1,0:T(8,128)(2,1)S(1)}, bf16[4,64,512]{2,1,0:T(8,128)(2,1)}, u32[]{:S(2)}) copy-start(bf16[4,64,512]{2,1,0:T(8,128)(2,1)} %gather_fusion.10) | copy-start | bytes 786436
  56.7 1.1 %copy-start.5 = (bf16[4,64,512]{2,1,0:T(8,128)(2,1)S(1)}, bf16[4,64,512]{2,1,0:T(8,128)(2,1)}, u32[]{:S(2)}) copy-start(bf16[4,64,512]{2,1,0:T(8,128)(2,1)} %gather_fusion.17) | copy-start | bytes 786436
  57.9 1.0 copy-start.6
  57.9 1.0 %copy-start.7 = (bf16[512,256]{1,0:T(8,128)(2,1)S(1)}, bf16[512,256]{1,0:T(8,128)(2,1)}, u32[]{:S(2)}) copy-start(bf16[512,256]{1,0:T(8,128)(2,1)} %reshape.68) | copy-start | bytes 786436
  59.5 15.1 %copy-start.12 = (f32[256]{0:T(256)S(1)}, f32[256]{0:T(256)}, u32[]{:S(2)}) copy-start(f32[256]{0:T(256)} %param.13) | copy-start | bytes 3076
  73.0 1.8 %copy-start.8 = (bf16[256,256]{1,0:T(8,128)(2,1)S(1)}, bf16[256,256]{1,0:T(8,128)(2,1)}, u32[]{:S(2)}) copy-start(bf16[256,256]{1,0:T(8,128)(2,1)} %param.14) | copy-start | bytes 393220
  73.4 2.0 %copy-start.9 = (bf16[256,256]{1,0:T(8,128)(2,1)S(1)}, bf16[256,256]{1,0:T(8,128)(2,1)}, u32[]{:S(2)}) copy-start(bf16[256,256]{1,0:T(8,128)(2,1)} %param.15) | copy-start | bytes 393220
  74.8 3.3 %copy-start.10 = (bf16[256,256]{1,0:T(8,128)(2,1)S(1)}, bf16[256,256]{1,0:T(8,128)(2,1)}, u32[]{:S(2)}) copy-start(bf16[256,256]{1,0:T(8,128)(2,1)} %param.16) | copy-start | bytes 393220
  86.5 1.0 %copy-start.11 = (bf16[256,256]{1,0:T(8,128)(2,1)S(1)}, bf16[256,256]{1,0:T(8,128)(2,1)}, u32[]{:S(2)}) copy-start(bf16[256,256]{1,0:T(8,128)(2,1)} %param.17) | copy-start | bytes 393220
where the time goes:
time: 99.5 us; the launch traced here: 98.8 us
  local copies, waits for them, and re-layouts  29.7 us (30%)
  blocking collectives  23.5 us (24%)
  matrix products  23.2 us (23%)
  starting transfers between devices  11.5 us (12%)
  waiting for transfers between devices  8.82 us (9%)
  other arithmetic  1.55 us (2%)
    gather x18, local copies, waits for them, and re-layouts, apply_tiles(): chosen = jnp.take(source, sources_at[:, slot], axis=0, mode='clip')  17.2 us
    dot_general x18, matrix products, apply_tiles(): jnp.einsum('gab,gbf->gaf', tile_blocks[:, slot], chosen, preferred_elemen...  15.4 us
    all_to_all x1, blocking collectives, on_device(): lax.all_to_all(grouped, 'tm', split_axis=0, concat_axis=2, tiled=True)  13.5 us
    all_to_all x1, blocking collectives, on_device(): lax.all_to_all(attended, 'tm', split_axis=2, concat_axis=0, tiled=True)  10.1 us
    ppermute x2, waiting for transfers between devices, with_halo(): lax.ppermute(lax.slice_in_dim(block, 0, width, axis=dim), axis, backward)  8.82 us
    ppermute x2, starting transfers between devices, with_halo(): lax.ppermute(lax.slice_in_dim(block, block.shape[dim] - width, None, axis...  7.12 us
    ppermute x2, starting transfers between devices, with_halo(): lax.ppermute(lax.slice_in_dim(block, 0, width, axis=dim), axis, backward)  4.33 us
    sub x1, matrix products, attend_group(): weights = jax.nn.softmax(scores, axis=-1).astype(jnp.bfloat16)  2.57 us
  transfers between devices with their start and end apart: 4, of which 2 were waited for; matrix products, arithmetic and copies ran while one was open for 4% of the time, Pallas kernels for 0%

commit v1 on v0

v1 whole, which is shorter than its diff:
```python
import math

import jax
import jax.numpy as jnp
from jax import lax
from jax.experimental import pallas as pl
from jax.experimental.pallas import tpu as pltpu
from jax.sharding import PartitionSpec as P

HEADS = 8
REACH = 2
GROUP = 8
MESH = pl.DeviceIdType.MESH
BF16 = jnp.bfloat16
F32 = jnp.float32


def matmul(left, right):
    return jnp.dot(left, right, preferred_element_type=F32)


def kernel(
    nbr_ref, x_ref, tiles_ref, cheb_ref, gain_ref, wq_ref, wk_ref, wv_ref, wo_ref, out_ref,
    band, first_buf, halo1, halo2, mixed_buf, gathered, back_send, back,
    h1_send, h1_recv, h2_send, h2_recv, a_send, a_recv, b_send, b_recv,
):
    pix_n, tm_n = lax.axis_size("pix"), lax.axis_size("tm")
    pix, tm = lax.axis_index("pix"), lax.axis_index("tm")
    right = lax.rem(pix + 1, pix_n)
    left = lax.rem(pix + pix_n - 1, pix_n)
    own_blocks, slots, tile, _ = tiles_ref.shape
    rows, features = x_ref.shape
    edge = REACH * tile
    channels = cheb_ref.shape[1]
    own_times = features // channels
    times = own_times * tm_n
    share = rows // tm_n

    barrier = pltpu.get_barrier_semaphore()
    for side in (left, right):
        pl.semaphore_signal(barrier, inc=1, device_id={"pix": side}, device_id_type=MESH)
    for k in range(1, tm_n):
        pl.semaphore_signal(
            barrier, inc=1, device_id={"tm": lax.rem(tm + k, tm_n)}, device_id_type=MESH
        )
    pl.semaphore_wait(barrier, 2 + tm_n - 1)

    def halo(source, target, send, recv):
        copies = []
        for at, (side, start, land) in enumerate(
            ((right, rows - edge, 0), (left, 0, edge))
        ):
            copies.append(
                pltpu.make_async_remote_copy(
                    src_ref=source.at[pl.ds(start, edge), :],
                    dst_ref=target.at[pl.ds(land, edge), :],
                    send_sem=send.at[at],
                    recv_sem=recv.at[at],
                    device_id={"pix": side},
                    device_id_type=MESH,
                )
            )
        for copy in copies:
            copy.start()
        return copies

    first_halo = halo(x_ref, halo1, h1_send, h1_recv)

    base = pix * own_blocks
    wide = own_blocks + 2 * REACH
    order = list(range(REACH, REACH + own_blocks)) + list(range(REACH)) + list(
        range(REACH + own_blocks, wide)
    )
    for g in range(own_blocks):
        spots = [nbr_ref[j, base + g] - base + REACH for j in range(slots)]
        held = [tiles_ref[g, j].astype(F32) for j in range(slots)]

        def entry(e):
            off = e - g
            if off < 0 or off > 2 * REACH:
                return jnp.zeros((tile, tile), F32)
            span = 2 * REACH + 1
            used = range(slots) if off == REACH else [off] + list(range(span, slots))
            total = None
            for j in used:
                term = held[j] * jnp.where(spots[j] == e, 1.0, 0.0).astype(F32)
                total = term if total is None else total + term
            return total

        for at in range(0, wide, 2):
            pair = jnp.concatenate([entry(order[at]), entry(order[at + 1])], axis=1)
            band[g * tile : (g + 1) * tile, at * tile : (at + 2) * tile] = pair.astype(BF16)

    signal = x_ref[...]
    own_first = matmul(band[:, :rows], signal)
    for copy in first_halo:
        copy.wait()
    first = (own_first + matmul(band[:, rows:], halo1[...])).astype(BF16)
    first_buf[...] = first
    second_halo = halo(first_buf, halo2, h2_send, h2_recv)

    own_second = matmul(band[:, :rows], first)
    partial = [
        matmul(signal[:, t * channels : (t + 1) * channels], cheb_ref[0])
        + matmul(first[:, t * channels : (t + 1) * channels], cheb_ref[1])
        for t in range(own_times)
    ]
    for copy in second_halo:
        copy.wait()
    wide_signal = signal.astype(F32)
    second = (
        2.0 * (own_second + matmul(band[:, rows:], halo2[...])) - wide_signal
    ).astype(BF16)
    for t in range(own_times):
        lanes = slice(t * channels, (t + 1) * channels)
        mixing = partial[t] + matmul(second[:, lanes], cheb_ref[2])
        mixed = wide_signal[:, lanes] + mixing / (1.0 + jnp.exp(-mixing))
        mixed_buf[:, lanes] = mixed.astype(BF16)

    out_copies = []
    for k in range(1, tm_n):
        peer = lax.rem(tm + k, tm_n)
        out_copies.append(
            pltpu.make_async_remote_copy(
                src_ref=mixed_buf.at[pl.ds(pl.multiple_of(peer * share, share), share), :],
                dst_ref=gathered.at[tm],
                send_sem=a_send.at[k - 1],
                recv_sem=a_recv.at[k - 1],
                device_id={"tm": peer},
                device_id_type=MESH,
            )
        )
    for copy in out_copies:
        copy.start()
    mine = pl.ds(pl.multiple_of(tm * share, share), share)
    gathered[tm] = mixed_buf[mine, :]
    for copy in out_copies:
        copy.wait()

    pieces = []
    for source in range(tm_n):
        piece = gathered[source].astype(F32)
        for t in range(own_times):
            pieces.append(piece[:, t * channels : (t + 1) * channels])
    flat = jnp.concatenate(pieces, axis=0)
    scaling = lax.rsqrt(jnp.mean(flat * flat, axis=1, keepdims=True) + 1e-06)
    normed = (flat * scaling * gain_ref[...]).astype(BF16)
    query = matmul(normed, wq_ref[...]).reshape(times, share, channels)
    keys = matmul(normed, wk_ref[...]).reshape(times, share, channels)
    values = matmul(normed, wv_ref[...]).reshape(times, share, channels)

    head_dim = channels // HEADS
    lane = lax.broadcasted_iota(jnp.int32, (1, channels), 1)
    head_masks = [
        jnp.where((lane >= h * head_dim) & (lane < (h + 1) * head_dim), 1.0, 0.0).astype(F32)
        for h in range(HEADS)
    ]
    count = times * GROUP
    row_pixel = lax.broadcasted_iota(jnp.int32, (HEADS * count, count), 0) & (GROUP - 1)
    col_pixel = lax.broadcasted_iota(jnp.int32, (HEADS * count, count), 1) & (GROUP - 1)
    same = row_pixel == col_pixel
    attended = []
    for group in range(share // GROUP):
        pick = slice(group * GROUP, (group + 1) * GROUP)
        q = query[:, pick].reshape(count, channels)
        k = keys[:, pick].reshape(count, channels).astype(BF16)
        v = values[:, pick].reshape(count, channels).astype(BF16)
        stacked = jnp.concatenate([(q * m).astype(BF16) for m in head_masks], axis=0)
        scores = lax.dot_general(
            stacked, k, (((1,), (1,)), ((), ())), preferred_element_type=F32
        ) * (1.0 / math.sqrt(head_dim))
        scores = jnp.where(same, scores, -jnp.inf)
        top = jnp.max(scores, axis=1, keepdims=True)
        weights = jnp.exp(scores - top)
        norm = jnp.sum(weights, axis=1, keepdims=True)
        product = matmul(weights.astype(BF16), v) / norm
        total = None
        for h in range(HEADS):
            term = product[h * count : (h + 1) * count] * head_masks[h]
            total = term if total is None else total + term
        attended.append(total.reshape(times, GROUP, channels))
    joined = jnp.concatenate(attended, axis=1).reshape(times * share, channels).astype(BF16)
    result = flat + matmul(joined, wo_ref[...])
    for t in range(times):
        lanes = slice((t % own_times) * channels, (t % own_times + 1) * channels)
        back_send[t // own_times, :, lanes] = result[t * share : (t + 1) * share].astype(BF16)

    back_copies = []
    for k in range(1, tm_n):
        peer = lax.rem(tm + k, tm_n)
        back_copies.append(
            pltpu.make_async_remote_copy(
                src_ref=back_send.at[peer],
                dst_ref=back.at[tm],
                send_sem=b_send.at[k - 1],
                recv_sem=b_recv.at[k - 1],
                device_id={"tm": peer},
                device_id_type=MESH,
            )
        )
    for copy in back_copies:
        copy.start()
    back[tm] = back_send[tm]
    for copy in back_copies:
        copy.wait()
    for source in range(tm_n):
        out_ref[source * share : (source + 1) * share, :] = back[source]


def on_device(
    signal, lap_tiles, neighbours, cheb_weight, norm_gain, w_query, w_key, w_value, w_out
):
    pix_count, time_count, channels = signal.shape
    tm_n = lax.axis_size("tm")
    tile = lap_tiles.shape[2]
    features = time_count * channels
    share = pix_count // tm_n
    halo_rows = 2 * REACH * tile
    vmem = pl.BlockSpec(memory_space=pltpu.VMEM)
    dma = pltpu.SemaphoreType.DMA
    out = pl.pallas_call(
        kernel,
        out_shape=jax.ShapeDtypeStruct((pix_count, features), BF16),
        in_specs=[pl.BlockSpec(memory_space=pltpu.SMEM)] + [vmem] * 8,
        out_specs=vmem,
        scratch_shapes=[
            pltpu.VMEM((pix_count, pix_count + halo_rows), BF16),
            pltpu.VMEM((pix_count, features), BF16),
            pltpu.VMEM((halo_rows, features), BF16),
            pltpu.VMEM((halo_rows, features), BF16),
            pltpu.VMEM((pix_count, features), BF16),
            pltpu.VMEM((tm_n, share, features), BF16),
            pltpu.VMEM((tm_n, share, features), BF16),
            pltpu.VMEM((tm_n, share, features), BF16),
            dma((2,)),
            dma((2,)),
            dma((2,)),
            dma((2,)),
            dma((tm_n - 1,)),
            dma((tm_n - 1,)),
            dma((tm_n - 1,)),
            dma((tm_n - 1,)),
        ],
        compiler_params=pltpu.CompilerParams(
            collective_id=0, has_side_effects=True, vmem_limit_bytes=48 << 20
        ),
        name="cheb_attend",
    )(
        neighbours.T,
        signal.reshape(pix_count, features),
        lap_tiles,
        cheb_weight,
        norm_gain.reshape(1, channels),
        w_query,
        w_key,
        w_value,
        w_out,
    )
    return out.reshape(pix_count, time_count, channels)


def solution(mesh):
    in_specs = (P("pix", "tm", None), P("pix", None, None, None), P(), P(), P(), P(), P(), P(), P())
    out_specs = P("pix", "tm", None)
    return jax.shard_map(
        on_device, mesh=mesh, in_specs=in_specs, out_specs=out_specs, check_vma=False
    )
```

time: 99.5 us -> 44.1 us (0.44)
  the two profiles are of different devices: /device:TPU:105 before, /device:TPU:4 now
where the time goes in v1:
time: 44.1 us; the launch traced here: 43.8 us
  Pallas kernels  36.8 us (83%)
  local copies, waits for them, and re-layouts  6.99 us (16%)
    pallas_call x1, Pallas kernels, on_device(): pl.pallas_call(kernel, out_shape=jax.ShapeDtypeStruct((pix_count, feature...  36.8 us
    unnamed x17, local copies, waits for them, and re-layouts  6.22 us

profile of v1, /device:TPU:4, one launch (start us, length us, event | category | flops | bytes accessed | tf_op | source)
XLA Modules:
  0.0 43.8 jit_solution(5217374972458379313)
XLA Ops:
  0.0 0.0 copy-start.1
  0.0 0.0 copy-start.2
  0.0 1.0 %copy.10 = bf16[32,8,2,256]{3,1,2,0:T(8,128)(2,1)S(1)} copy(bf16[32,8,2,256]{3,2,1,0:T(2,128)(2,1)} %bitcast.7) | data formatting | bytes 524288
  1.0 0.0 copy-start.7
  1.1 0.0 copy-done.1
  1.1 0.0 copy-done.2
  1.1 0.6 %copy-done.7 = f32[256]{0:T(256)S(1)} copy-done((f32[256]{0:T(256)S(1)}, f32[256]{0:T(256)}, u32[]{:S(2)}) %copy-start.7) | copy-done | bytes 1048
  1.7 0.0 copy-start
  1.7 1.1 %copy-done = bf16[4,9,64,64]{3,2,1,0:T(8,128)(2,1)S(1)} copy-done((bf16[4,9,64,64]{3,2,1,0:T(8,128)(2,1)S(1)}, bf16[4,9,64,64]{3,2,1,0:T(8,128)(2,1)}, u32[]{:S(2)}) %copy-start) | copy-done | bytes 294936
  2.8 0.0 copy-start.3
  2.8 0.9 %copy-done.3 = bf16[256,256]{1,0:T(8,128)(2,1)S(1)} copy-done((bf16[256,256]{1,0:T(8,128)(2,1)S(1)}, bf16[256,256]{1,0:T(8,128)(2,1)}, u32[]{:S(2)}) %copy-start.3) | copy-done | bytes 131096
  3.7 0.0 copy-start.4
  3.7 0.9 %copy-done.4 = bf16[256,256]{1,0:T(8,128)(2,1)S(1)} copy-done((bf16[256,256]{1,0:T(8,128)(2,1)S(1)}, bf16[256,256]{1,0:T(8,128)(2,1)}, u32[]{:S(2)}) %copy-start.4) | copy-done | bytes 131096
  4.6 0.0 copy-start.5
  4.6 0.9 %copy-done.5 = bf16[256,256]{1,0:T(8,128)(2,1)S(1)} copy-done((bf16[256,256]{1,0:T(8,128)(2,1)S(1)}, bf16[256,256]{1,0:T(8,128)(2,1)}, u32[]{:S(2)}) %copy-start.5) | copy-done | bytes 131096
  5.5 0.0 copy-start.6
  5.5 0.7 %copy-done.6 = s32[256,9]{0,1:T(8,128)S(1)} copy-done((s32[256,9]{0,1:T(8,128)S(1)}, s32[256,9]{0,1:T(8,128)}, u32[]{:S(2)}) %copy-start.6) | copy-done | bytes 9240
  6.2 36.8 %cheb_attend.1 = bf16[256,512]{1,0:T(8,128)(2,1)S(1)} custom-call(s32[9,256]{1,0:T(8,128)S(1)} %bitcast.5, bf16[256,512]{1,0:T(8,128)(2,1)S(1)} %bitcast.4, bf16[4,9,64,64]{3,2,1,0:T(8,128)(2,1)S(1)} %copy-done, bf16[3,256,256]{2,1,0:T(8,128)(2,1)S(1)} %copy-done.1, f32[1,256]{1,0:T(1,128)S(1)} %bitcast.6, bf16[256,256]{1,0:T(8,128)(2,1)S(1)} %copy-done.2, ...), custom_call_target="tpu_custom_call" | custom-call | tf_op jit(solution)/shard_map/cheb_attend/pallas_call | solution.py:221
  43.1 0.8 %reshape.11 = bf16[256,2,256]{2,1,0:T(2,128)(2,1)} reshape(bf16[256,512]{1,0:T(8,128)(2,1)S(1)} %cheb_attend.1) | data formatting | bytes 524288 | tf_op jit(solution)/shard_map/reshape | solution.py:259
Async XLA Ops:
  0.0 1.1 %copy-start.1 = (bf16[3,256,256]{2,1,0:T(8,128)(2,1)S(1)}, bf16[3,256,256]{2,1,0:T(8,128)(2,1)}, u32[]{:S(2)}) copy-start(bf16[3,256,256]{2,1,0:T(8,128)(2,1)} %cheb_ref.1) | copy-start | bytes 1179652
  0.0 1.1 %copy-start.2 = (bf16[256,256]{1,0:T(8,128)(2,1)S(1)}, bf16[256,256]{1,0:T(8,128)(2,1)}, u32[]{:S(2)}) copy-start(bf16[256,256]{1,0:T(8,128)(2,1)} %wq_ref.1) | copy-start | bytes 393220
  1.0 0.7 %copy-start.7 = (f32[256]{0:T(256)S(1)}, f32[256]{0:T(256)}, u32[]{:S(2)}) copy-start(f32[256]{0:T(256)} %param.13) | copy-start | bytes 3076
  1.7 1.1 %copy-start = (bf16[4,9,64,64]{3,2,1,0:T(8,128)(2,1)S(1)}, bf16[4,9,64,64]{3,2,1,0:T(8,128)(2,1)}, u32[]{:S(2)}) copy-start(bf16[4,9,64,64]{3,2,1,0:T(8,128)(2,1)} %tiles_ref.1) | copy-start | bytes 884740
  2.8 0.9 %copy-start.3 = (bf16[256,256]{1,0:T(8,128)(2,1)S(1)}, bf16[256,256]{1,0:T(8,128)(2,1)}, u32[]{:S(2)}) copy-start(bf16[256,256]{1,0:T(8,128)(2,1)} %wk_ref.1) | copy-start | bytes 393220
  3.7 0.9 %copy-start.4 = (bf16[256,256]{1,0:T(8,128)(2,1)S(1)}, bf16[256,256]{1,0:T(8,128)(2,1)}, u32[]{:S(2)}) copy-start(bf16[256,256]{1,0:T(8,128)(2,1)} %wv_ref.1) | copy-start | bytes 393220
  4.6 0.9 %copy-start.5 = (bf16[256,256]{1,0:T(8,128)(2,1)S(1)}, bf16[256,256]{1,0:T(8,128)(2,1)}, u32[]{:S(2)}) copy-start(bf16[256,256]{1,0:T(8,128)(2,1)} %wo_ref.1) | copy-start | bytes 393220
  5.5 0.7 %copy-start.6 = (s32[256,9]{0,1:T(8,128)S(1)}, s32[256,9]{0,1:T(8,128)}, u32[]{:S(2)}) copy-start(s32[256,9]{0,1:T(8,128)} %param.11) | copy-start | bytes 27652

commit v2 on v1

v2 whole, which is shorter than its diff:
```python
import math

import jax
import jax.numpy as jnp
from jax import lax
from jax.experimental import pallas as pl
from jax.experimental.pallas import tpu as pltpu
from jax.sharding import PartitionSpec as P

HEADS = 8
REACH = 2
GROUP = 8
CHUNKS = 2
MESH = pl.DeviceIdType.MESH
BF16 = jnp.bfloat16
F32 = jnp.float32


def matmul(left, right):
    return jnp.dot(left, right, preferred_element_type=F32)


def kernel(
    nbr_hbm, x_hbm, tiles_hbm, cheb_hbm, gain_hbm, wq_hbm, wk_hbm, wv_hbm, wo_hbm, out_ref,
    nbr_ref, x_ref, tiles_ref, cheb_ref, gain_ref, wq_ref, wk_ref, wv_ref, wo_ref,
    band, first_buf, halo1, halo2, mixed_buf, gathered, back_send, back,
    load_sem, h1_send, h1_recv, h2_send, h2_recv, a_send, a_recv, b_send, b_recv,
):
    pix_n, tm_n = lax.axis_size("pix"), lax.axis_size("tm")
    pix, tm = lax.axis_index("pix"), lax.axis_index("tm")
    right = lax.rem(pix + 1, pix_n)
    left = lax.rem(pix + pix_n - 1, pix_n)
    own_blocks, slots, tile, _ = tiles_ref.shape
    own_times, rows, channels = x_ref.shape
    edge = REACH * tile
    times = own_times * tm_n
    share = rows // tm_n
    part = share // CHUNKS

    loads = [
        pltpu.make_async_copy(source, target, load_sem.at[at])
        for at, (source, target) in enumerate(
            (
                (nbr_hbm, nbr_ref), (tiles_hbm, tiles_ref), (x_hbm, x_ref),
                (cheb_hbm, cheb_ref), (gain_hbm, gain_ref), (wq_hbm, wq_ref), (wk_hbm, wk_ref),
                (wv_hbm, wv_ref), (wo_hbm, wo_ref),
            )
        )
    ]
    for load in loads:
        load.start()

    barrier = pltpu.get_barrier_semaphore()
    for side in (left, right):
        pl.semaphore_signal(barrier, inc=1, device_id={"pix": side}, device_id_type=MESH)
    for k in range(1, tm_n):
        pl.semaphore_signal(
            barrier, inc=1, device_id={"tm": lax.rem(tm + k, tm_n)}, device_id_type=MESH
        )
    pl.semaphore_wait(barrier, 2 + tm_n - 1)

    sent = []

    def halo(source, target, send, recv, t):
        copies = []
        for at, (side, start, land) in enumerate(
            ((right, rows - edge, 0), (left, 0, edge))
        ):
            copies.append(
                pltpu.make_async_remote_copy(
                    src_ref=source.at[t, pl.ds(start, edge), :],
                    dst_ref=target.at[t, pl.ds(land, edge), :],
                    send_sem=send.at[t, at],
                    recv_sem=recv.at[t, at],
                    device_id={"pix": side},
                    device_id_type=MESH,
                )
            )
        for copy in copies:
            copy.start()
        sent.extend(copies)
        return copies

    first_halo = [halo(x_hbm, halo1, h1_send, h1_recv, t) for t in range(own_times)]

    loads[0].wait()
    loads[1].wait()
    base = pix * own_blocks
    wide = own_blocks + 2 * REACH
    order = list(range(REACH, REACH + own_blocks)) + list(range(REACH)) + list(
        range(REACH + own_blocks, wide)
    )
    for g in range(own_blocks):
        spots = [nbr_ref[j, base + g] - base + REACH for j in range(slots)]
        held = [tiles_ref[g, j].astype(F32) for j in range(slots)]

        def entry(e):
            off = e - g
            if off < 0 or off > 2 * REACH:
                return jnp.zeros((tile, tile), F32)
            span = 2 * REACH + 1
            used = range(slots) if off == REACH else [off] + list(range(span, slots))
            total = None
            for j in used:
                term = held[j] * jnp.where(spots[j] == e, 1.0, 0.0).astype(F32)
                total = term if total is None else total + term
            return total

        for at in range(0, wide, 2):
            pair = jnp.concatenate([entry(order[at]), entry(order[at + 1])], axis=1)
            band[g * tile : (g + 1) * tile, at * tile : (at + 2) * tile] = pair.astype(BF16)

    for load in loads[2:]:
        load.wait()
    own_first = [matmul(band[:, :rows], x_ref[t]) for t in range(own_times)]
    second_halo = []
    for t in range(own_times):
        for copy in first_halo[t]:
            copy.wait_recv()
        first_buf[t] = (own_first[t] + matmul(band[:, rows:], halo1[t])).astype(BF16)
        second_halo.append(halo(first_buf, halo2, h2_send, h2_recv, t))

    own_second = [matmul(band[:, :rows], first_buf[t]) for t in range(own_times)]
    partial = [
        matmul(x_ref[t], cheb_ref[0]) + matmul(first_buf[t], cheb_ref[1])
        for t in range(own_times)
    ]
    arriving = []
    for t in range(own_times):
        for copy in second_halo[t]:
            copy.wait_recv()
        wide_signal = x_ref[t].astype(F32)
        second = (
            2.0 * (own_second[t] + matmul(band[:, rows:], halo2[t])) - wide_signal
        ).astype(BF16)
        mixing = partial[t] + matmul(second, cheb_ref[2])
        mixed = wide_signal + mixing / (1.0 + jnp.exp(-mixing))
        mixed_buf[t] = mixed.astype(BF16)
        for c in range(CHUNKS):
            for k in range(1, tm_n):
                peer = lax.rem(tm + k, tm_n)
                start = pl.multiple_of(peer * share + c * part, part)
                copy = pltpu.make_async_remote_copy(
                    src_ref=mixed_buf.at[t, pl.ds(start, part), :],
                    dst_ref=gathered.at[c, tm, t],
                    send_sem=a_send.at[t, c, k - 1],
                    recv_sem=a_recv.at[t, c, k - 1],
                    device_id={"tm": peer},
                    device_id_type=MESH,
                )
                copy.start()
                arriving.append((c, copy))
                sent.append(copy)
        for c in range(CHUNKS):
            start = pl.multiple_of(tm * share + c * part, part)
            gathered[c, tm, t] = mixed_buf[t, pl.ds(start, part), :]

    head_dim = channels // HEADS
    lane = lax.broadcasted_iota(jnp.int32, (1, channels), 1)
    head_masks = [
        jnp.where((lane >= h * head_dim) & (lane < (h + 1) * head_dim), 1.0, 0.0).astype(F32)
        for h in range(HEADS)
    ]
    count = times * GROUP
    row_pixel = lax.broadcasted_iota(jnp.int32, (HEADS * count, count), 0) & (GROUP - 1)
    col_pixel = lax.broadcasted_iota(jnp.int32, (HEADS * count, count), 1) & (GROUP - 1)
    same = row_pixel == col_pixel
    returning = []
    for c in range(CHUNKS):
        for chunk, copy in arriving:
            if chunk == c:
                copy.wait_recv()
        flat = jnp.concatenate(
            [gathered[c, s, t].astype(F32) for s in range(tm_n) for t in range(own_times)],
            axis=0,
        )
        scaling = lax.rsqrt(jnp.mean(flat * flat, axis=1, keepdims=True) + 1e-06)
        normed = (flat * scaling * gain_ref[...]).astype(BF16)
        query = matmul(normed, wq_ref[...]).reshape(times, part, channels)
        keys = matmul(normed, wk_ref[...]).reshape(times, part, channels)
        values = matmul(normed, wv_ref[...]).reshape(times, part, channels)
        attended = []
        for group in range(part // GROUP):
            pick = slice(group * GROUP, (group + 1) * GROUP)
            q = query[:, pick].reshape(count, channels)
            k = keys[:, pick].reshape(count, channels).astype(BF16)
            v = values[:, pick].reshape(count, channels).astype(BF16)
            stacked = jnp.concatenate([(q * m).astype(BF16) for m in head_masks], axis=0)
            scores = lax.dot_general(
                stacked, k, (((1,), (1,)), ((), ())), preferred_element_type=F32
            ) * (1.0 / math.sqrt(head_dim))
            scores = jnp.where(same, scores, -jnp.inf)
            top = jnp.max(scores, axis=1, keepdims=True)
            weights = jnp.exp(scores - top)
            norm = jnp.sum(weights, axis=1, keepdims=True)
            product = matmul(weights.astype(BF16), v) / norm
            total = None
            for h in range(HEADS):
                term = product[h * count : (h + 1) * count] * head_masks[h]
                total = term if total is None else total + term
            attended.append(total.reshape(times, GROUP, channels))
        joined = jnp.concatenate(attended, axis=1).reshape(times * part, channels)
        result = flat + matmul(joined.astype(BF16), wo_ref[...])
        for t in range(times):
            back_send[c, t // own_times, t % own_times] = result[
                t * part : (t + 1) * part
            ].astype(BF16)
        for k in range(1, tm_n):
            peer = lax.rem(tm + k, tm_n)
            copy = pltpu.make_async_remote_copy(
                src_ref=back_send.at[c, peer],
                dst_ref=back.at[c, tm],
                send_sem=b_send.at[c, k - 1],
                recv_sem=b_recv.at[c, k - 1],
                device_id={"tm": peer},
                device_id_type=MESH,
            )
            copy.start()
            returning.append((c, copy))
            sent.append(copy)
        back[c, tm] = back_send[c, tm]

    for c in range(CHUNKS):
        for chunk, copy in returning:
            if chunk == c:
                copy.wait_recv()
        for s in range(tm_n):
            for t in range(own_times):
                start = s * share + c * part
                out_ref[t, start : start + part, :] = back[c, s, t]
    for copy in sent:
        copy.wait_send()


def on_device(
    signal, lap_tiles, neighbours, cheb_weight, norm_gain, w_query, w_key, w_value, w_out
):
    pix_count, time_count, channels = signal.shape
    tm_n = lax.axis_size("tm")
    tile = lap_tiles.shape[2]
    share = pix_count // tm_n
    part = share // CHUNKS
    halo_rows = 2 * REACH * tile
    vmem = pl.BlockSpec(memory_space=pltpu.VMEM)
    hbm = pl.BlockSpec(memory_space=pltpu.HBM)
    dma = pltpu.SemaphoreType.DMA
    operands = (
        neighbours.T,
        signal.transpose(1, 0, 2),
        lap_tiles,
        cheb_weight,
        norm_gain.reshape(1, channels),
        w_query,
        w_key,
        w_value,
        w_out,
    )
    local = [pltpu.SMEM(operands[0].shape, jnp.int32)] + [
        pltpu.VMEM(operand.shape, operand.dtype) for operand in operands[1:]
    ]
    slab = (time_count, pix_count, channels)
    halo_slab = (time_count, halo_rows, channels)
    exchange = (CHUNKS, tm_n, time_count, part, channels)
    out = pl.pallas_call(
        kernel,
        out_shape=jax.ShapeDtypeStruct(slab, BF16),
        in_specs=[hbm] * 9,
        out_specs=vmem,
        scratch_shapes=local
        + [
            pltpu.VMEM((pix_count, pix_count + halo_rows), BF16),
            pltpu.VMEM(slab, BF16),
            pltpu.VMEM(halo_slab, BF16),
            pltpu.VMEM(halo_slab, BF16),
            pltpu.VMEM(slab, BF16),
            pltpu.VMEM(exchange, BF16),
            pltpu.VMEM(exchange, BF16),
            pltpu.VMEM(exchange, BF16),
            dma((9,)),
        ]
        + [dma((time_count, 2))] * 4
        + [dma((time_count, CHUNKS, tm_n - 1))] * 2
        + [dma((CHUNKS, tm_n - 1))] * 2,
        compiler_params=pltpu.CompilerParams(
            collective_id=0, has_side_effects=True
        ),
        name="cheb_attend",
    )(*operands)
    return out.transpose(1, 0, 2)


def solution(mesh):
    in_specs = (P("pix", "tm", None), P("pix", None, None, None), P(), P(), P(), P(), P(), P(), P())
    out_specs = P("pix", "tm", None)
    return jax.shard_map(
        on_device, mesh=mesh, in_specs=in_specs, out_specs=out_specs, check_vma=False
    )
```

time: 44.1 us -> 39.4 us (0.89)
  local copies, waits for them, and re-layouts: 6.99 us -> 3.6 us
  Pallas kernels: 36.8 us -> 35.6 us
    unnamed x17 -> x1, local copies, waits for them, and re-layouts: 6.22 us -> 1.68 us
    transpose x0 -> x1, local copies, waits for them, and re-layouts: none -> 1.92 us  [on_device(): return out.transpose(1, 0, 2)]
    pallas_call x1, Pallas kernels: 36.8 us -> 35.6 us  [on_device(): pl.pallas_call(kernel, out_shape=jax.ShapeDtypeStruct(slab, BF16), in_spe...]
    reshape x1 -> x0, local copies, waits for them, and re-layouts: 0.77 us -> none  [on_device(): return out.reshape(pix_count, time_count, channels)]
where the time goes in v2:
time: 39.4 us; the launch traced here: 39.2 us
  Pallas kernels  35.6 us (90%)
  local copies, waits for them, and re-layouts  3.6 us (9%)
    pallas_call x1, Pallas kernels, on_device(): pl.pallas_call(kernel, out_shape=jax.ShapeDtypeStruct(slab, BF16), in_spe...  35.6 us
    transpose x1, local copies, waits for them, and re-layouts, on_device(): return out.transpose(1, 0, 2)  1.92 us
    unnamed x1, local copies, waits for them, and re-layouts  1.68 us

profile of v2, /device:TPU:4, one launch (start us, length us, event | category | flops | bytes accessed | tf_op | source)
XLA Modules:
  0.0 39.2 jit_solution(5769584306396354191)
XLA Ops:
  0.0 1.7 %copy.13 = bf16[256,2,256]{2,0,1:T(8,128)(2,1)} copy(bf16[256,2,256]{2,1,0:T(2,128)(2,1)} %param.9) | data formatting | bytes 524288 | tf_op args[0]
  1.7 35.6 %cheb_attend.1 = bf16[2,256,256]{2,1,0:T(8,128)(2,1)} custom-call(s32[9,256]{1,0:T(8,128)} %bitcast.8, bf16[2,256,256]{2,1,0:T(8,128)(2,1)} %bitcast.7, bf16[4,9,64,64]{3,2,1,0:T(8,128)(2,1)} %tiles_hbm.1, bf16[3,256,256]{2,1,0:T(8,128)(2,1)} %cheb_hbm.1, f32[1,256]{1,0:T(1,128)} %bitcast.9, bf16[256,256]{1,0:T(8,128)(2,1)} %wq_hbm.1, ...), custom_call_target="tpu_custom_call" | custom-call | tf_op jit(solution)/shard_map/cheb_attend/pallas_call | solution.py:264
  37.3 1.9 %copy.11 = bf16[256,2,256]{2,1,0:T(2,128)(2,1)} copy(bf16[256,2,256]{2,0,1:T(8,128)(2,1)} %bitcast.6) | data formatting | bytes 524288 | tf_op jit(solution)/shard_map/transpose | solution.py:289

commit v3 on v2

--- a/solution.py
+++ b/solution.py
@@ -51,15 +51,31 @@
         load.start()
 
     barrier = pltpu.get_barrier_semaphore()
-    for side in (left, right):
-        pl.semaphore_signal(barrier, inc=1, device_id={"pix": side}, device_id_type=MESH)
+    has_left, has_right = pix > 0, pix < pix_n - 1
+    for side, present in ((left, has_left), (right, has_right)):
+
+        @pl.when(present)
+        def _():
+            pl.semaphore_signal(barrier, inc=1, device_id={"pix": side}, device_id_type=MESH)
+
     for k in range(1, tm_n):
         pl.semaphore_signal(
             barrier, inc=1, device_id={"tm": lax.rem(tm + k, tm_n)}, device_id_type=MESH
         )
-    pl.semaphore_wait(barrier, 2 + tm_n - 1)
-
-    sent = []
+    present_count = jnp.minimum(pix, 1) + jnp.minimum(pix_n - 1 - pix, 1)
+    pl.semaphore_wait(barrier, present_count + tm_n - 1)
+
+    @pl.when(jnp.logical_not(has_left))
+    def _():
+        for buffer in (halo1, halo2):
+            buffer[:, :edge] = jnp.zeros((own_times, edge, channels), BF16)
+
+    @pl.when(jnp.logical_not(has_right))
+    def _():
+        for buffer in (halo1, halo2):
+            buffer[:, edge:] = jnp.zeros((own_times, edge, channels), BF16)
+
+    sent, halos = [], []
 
     def halo(source, target, send, recv, t):
         copies = []
@@ -76,10 +92,14 @@
                     device_id_type=MESH,
                 )
             )
-        for copy in copies:
-            copy.start()
-        sent.extend(copies)
+        pl.when(has_right)(copies[0].start)
+        pl.when(has_left)(copies[1].start)
+        halos.append(copies)
         return copies
+
+    def halo_arrives(copies):
+        pl.when(has_left)(copies[0].wait_recv)
+        pl.when(has_right)(copies[1].wait_recv)
 
     first_halo = [halo(x_hbm, halo1, h1_send, h1_recv, t) for t in range(own_times)]
 
@@ -115,8 +135,7 @@
     own_first = [matmul(band[:, :rows], x_ref[t]) for t in range(own_times)]
     second_halo = []
     for t in range(own_times):
-        for copy in first_halo[t]:
-            copy.wait_recv()
+        halo_arrives(first_halo[t])
         first_buf[t] = (own_first[t] + matmul(band[:, rows:], halo1[t])).astype(BF16)
         second_halo.append(halo(first_buf, halo2, h2_send, h2_recv, t))
 
@@ -127,8 +146,7 @@
     ]
     arriving = []
     for t in range(own_times):
-        for copy in second_halo[t]:
-            copy.wait_recv()
+        halo_arrives(second_halo[t])
         wide_signal = x_ref[t].astype(F32)
         second = (
             2.0 * (own_second[t] + matmul(band[:, rows:], halo2[t])) - wide_signal
@@ -228,6 +246,9 @@
             for t in range(own_times):
                 start = s * share + c * part
                 out_ref[t, start : start + part, :] = back[c, s, t]
+    for to_right, to_left in halos:
+        pl.when(has_right)(to_right.wait_send)
+        pl.when(has_left)(to_left.wait_send)
     for copy in sent:
         copy.wait_send()
 

time: 39.4 us -> 35.1 us (0.89)
  the two profiles are of different devices: /device:TPU:4 before, /device:TPU:8 now
where the time goes in v3:
time: 35.1 us; the launch traced here: 34.9 us
  Pallas kernels  31.3 us (89%)
  local copies, waits for them, and re-layouts  3.6 us (10%)
    pallas_call x1, Pallas kernels, on_device(): pl.pallas_call(kernel, out_shape=jax.ShapeDtypeStruct(slab, BF16), in_spe...  31.3 us
    transpose x1, local copies, waits for them, and re-layouts, on_device(): return out.transpose(1, 0, 2)  1.92 us
    unnamed x1, local copies, waits for them, and re-layouts  1.68 us

profile of v3, /device:TPU:8, one launch (start us, length us, event | category | flops | bytes accessed | tf_op | source)
XLA Modules:
  0.0 34.9 jit_solution(17277196390995578557)
XLA Ops:
  0.0 1.7 %copy.13 = bf16[256,2,256]{2,0,1:T(8,128)(2,1)} copy(bf16[256,2,256]{2,1,0:T(2,128)(2,1)} %param.9) | data formatting | bytes 524288 | tf_op args[0]
  1.7 31.3 %cheb_attend.1 = bf16[2,256,256]{2,1,0:T(8,128)(2,1)} custom-call(s32[9,256]{1,0:T(8,128)} %bitcast.8, bf16[2,256,256]{2,1,0:T(8,128)(2,1)} %bitcast.7, bf16[4,9,64,64]{3,2,1,0:T(8,128)(2,1)} %tiles_hbm.1, bf16[3,256,256]{2,1,0:T(8,128)(2,1)} %cheb_hbm.1, f32[1,256]{1,0:T(1,128)} %bitcast.9, bf16[256,256]{1,0:T(8,128)(2,1)} %wq_hbm.1, ...), custom_call_target="tpu_custom_call" | custom-call | tf_op jit(solution)/shard_map/cheb_attend/pallas_call | solution.py:285
  33.0 1.9 %copy.11 = bf16[256,2,256]{2,1,0:T(2,128)(2,1)} copy(bf16[256,2,256]{2,0,1:T(8,128)(2,1)} %bitcast.6) | data formatting | bytes 524288 | tf_op jit(solution)/shard_map/transpose | solution.py:310

commit v4 on v3

--- a/solution.py
+++ b/solution.py
@@ -22,8 +22,8 @@
 
 def kernel(
     nbr_hbm, x_hbm, tiles_hbm, cheb_hbm, gain_hbm, wq_hbm, wk_hbm, wv_hbm, wo_hbm, out_ref,
-    nbr_ref, x_ref, tiles_ref, cheb_ref, gain_ref, wq_ref, wk_ref, wv_ref, wo_ref,
-    band, first_buf, halo1, halo2, mixed_buf, gathered, back_send, back,
+    nbr_ref, x_pairs, tiles_ref, cheb_ref, gain_ref, wq_ref, wk_ref, wv_ref, wo_ref,
+    x_ref, band, first_buf, halo1, halo2, mixed_buf, gathered, back_send, back,
     load_sem, h1_send, h1_recv, h2_send, h2_recv, a_send, a_recv, b_send, b_recv,
 ):
     pix_n, tm_n = lax.axis_size("pix"), lax.axis_size("tm")
@@ -41,7 +41,7 @@
         pltpu.make_async_copy(source, target, load_sem.at[at])
         for at, (source, target) in enumerate(
             (
-                (nbr_hbm, nbr_ref), (tiles_hbm, tiles_ref), (x_hbm, x_ref),
+                (x_hbm, x_pairs), (nbr_hbm, nbr_ref), (tiles_hbm, tiles_ref),
                 (cheb_hbm, cheb_ref), (gain_hbm, gain_ref), (wq_hbm, wq_ref), (wk_hbm, wk_ref),
                 (wv_hbm, wv_ref), (wo_hbm, wo_ref),
             )
@@ -62,6 +62,9 @@
         pl.semaphore_signal(
             barrier, inc=1, device_id={"tm": lax.rem(tm + k, tm_n)}, device_id_type=MESH
         )
+    loads[0].wait()
+    for t in range(own_times):
+        x_ref[t] = x_pairs[:, t, :]
     present_count = jnp.minimum(pix, 1) + jnp.minimum(pix_n - 1 - pix, 1)
     pl.semaphore_wait(barrier, present_count + tm_n - 1)
 
@@ -101,10 +104,10 @@
         pl.when(has_left)(copies[0].wait_recv)
         pl.when(has_right)(copies[1].wait_recv)
 
-    first_halo = [halo(x_hbm, halo1, h1_send, h1_recv, t) for t in range(own_times)]
-
-    loads[0].wait()
+    first_halo = [halo(x_ref, halo1, h1_send, h1_recv, t) for t in range(own_times)]
+
     loads[1].wait()
+    loads[2].wait()
     base = pix * own_blocks
     wide = own_blocks + 2 * REACH
     order = list(range(REACH, REACH + own_blocks)) + list(range(REACH)) + list(
@@ -130,7 +133,7 @@
             pair = jnp.concatenate([entry(order[at]), entry(order[at + 1])], axis=1)
             band[g * tile : (g + 1) * tile, at * tile : (at + 2) * tile] = pair.astype(BF16)
 
-    for load in loads[2:]:
+    for load in loads[3:]:
         load.wait()
     own_first = [matmul(band[:, :rows], x_ref[t]) for t in range(own_times)]
     second_halo = []
@@ -267,7 +270,7 @@
     dma = pltpu.SemaphoreType.DMA
     operands = (
         neighbours.T,
-        signal.transpose(1, 0, 2),
+        signal,
         lap_tiles,
         cheb_weight,
         norm_gain.reshape(1, channels),
@@ -289,6 +292,7 @@
         out_specs=vmem,
         scratch_shapes=local
         + [
+            pltpu.VMEM(slab, BF16),
             pltpu.VMEM((pix_count, pix_count + halo_rows), BF16),
             pltpu.VMEM(slab, BF16),
             pltpu.VMEM(halo_slab, BF16),

time: 35.1 us -> 33.1 us (0.943)
  local copies, waits for them, and re-layouts: 3.6 us -> 1.92 us
    unnamed x1 -> x0, local copies, waits for them, and re-layouts: 1.68 us -> none
where the time goes in v4:
time: 33.1 us; the launch traced here: 33 us
  Pallas kernels  31.1 us (94%)
  local copies, waits for them, and re-layouts  1.92 us (6%)
    pallas_call x1, Pallas kernels, on_device(): pl.pallas_call(kernel, out_shape=jax.ShapeDtypeStruct(slab, BF16), in_spe...  31.1 us
    transpose x1, local copies, waits for them, and re-layouts, on_device(): return out.transpose(1, 0, 2)  1.92 us

profile of v4, /device:TPU:8, one launch (start us, length us, event | category | flops | bytes accessed | tf_op | source)
XLA Modules:
  0.0 33.0 jit_solution(12982798957246469211)
XLA Ops:
  0.0 31.1 %cheb_attend.1 = bf16[2,256,256]{2,1,0:T(8,128)(2,1)} custom-call(s32[9,256]{1,0:T(8,128)} %bitcast.4, bf16[256,2,256]{2,1,0:T(2,128)(2,1)} %x_hbm.1, bf16[4,9,64,64]{3,2,1,0:T(8,128)(2,1)} %tiles_hbm.1, bf16[3,256,256]{2,1,0:T(8,128)(2,1)} %cheb_hbm.1, f32[1,256]{1,0:T(1,128)} %bitcast.5, bf16[256,256]{1,0:T(8,128)(2,1)} %wq_hbm.1, ...), custom_call_target="tpu_custom_call" | custom-call | tf_op jit(solution)/shard_map/cheb_attend/pallas_call | solution.py:288
  31.1 1.9 %copy.10 = bf16[256,2,256]{2,1,0:T(2,128)(2,1)} copy(bf16[256,2,256]{2,0,1:T(8,128)(2,1)} %bitcast.3) | data formatting | bytes 524288 | tf_op jit(solution)/shard_map/transpose | solution.py:314
